TPU v7x, 256 devices: a whole 4x4x8 slice. The times are simulated.
256 devices in a mesh: dp: 4 (over y), mp: 16 (over x, z_lo), section: 4 (over z_hi, core).
Axes of the slice: x: 4, y: 4, z: 8 (z_hi: 2, z_lo: 4; z = z_hi * 4 + z_lo), core: 2. Of those that a mesh axis runs over, the one named last changes fastest.
Arguments:
- hidden_in: bfloat16 [64, 2560], P('dp', 'mp'), may hold values from -6 to 6
- lengths: int32 [64], P('dp'), may hold values from 0 to 7
- slots: int32 [64], P('dp'), may hold values from 0 to 71, as said below
- norm_gain: float32 [4, 2560], P('section'), may hold values from 0.5 to 1.5
- w_zxo: bfloat16 [4, 3, 5120, 2560], P('section', None, 'dp', 'mp'), may hold values from -0.125 to 0.125
- w_bcdt: bfloat16 [4, 336, 2560], P('section', 'dp', 'mp'), may hold values from -0.125 to 0.125
- conv_x_weight: float32 [4, 4, 5120], P('section', None, 'mp'), may hold values from -0.5 to 0.5
- conv_bc_weight: float32 [4, 4, 256], P('section'), may hold values from -0.5 to 0.5
- conv_x_pool: bfloat16 [4, 72, 3, 5120], P('section', 'dp', None, 'mp'), may hold values from -6 to 6
- conv_bc_pool: bfloat16 [4, 72, 3, 256], P('section', 'dp'), may hold values from -6 to 6
- state_pool: float32 [4, 72, 80, 64, 128], P('section', 'dp', 'mp'), may hold values from -1 to 1
- a_rate: float32 [4, 80], P('section', 'mp'), may hold values from 1 to 16
- dt_bias: float32 [4, 80], P('section', 'mp'), may hold values from -3 to 0
- skip_gain: float32 [4, 80], P('section', 'mp'), may hold values from 0.5 to 1.5
- gate_gain: float32 [4, 5120], P('section', 'mp'), may hold values from 0.5 to 1.5
Outputs:
- hidden_out: bfloat16 [4, 64, 2560], P('section', 'dp', 'mp')
- state_out: float32 [4, 64, 80, 64, 128], P('section', 'dp', 'mp')
Inputs may be any that keep to these rules, and one draw needn't show every extreme that they name: The sequences of the d-th block of 16 name distinct slots, all from d * 18 to (d + 1) * 18 - 1.
All inputs are finite; a program needn't handle non-finite values.
Results may differ from a plain program's by a relative error of at most 0.025.
Values may be sent and summed in bfloat16 or wider, within the bound.
A program may use at most 128 MiB of HBM per device.

v0:
```python
import jax
import jax.numpy as jnp
from jax import lax
from jax.sharding import PartitionSpec as P

MICRO = 4
epsilon = 1e-05


def copy_for_each(array, axis):
    devices = lax.axis_size(axis)
    return lax.all_to_all(
        jnp.broadcast_to(array[None], (devices, *array.shape)), axis, 0, 0, tiled=True
    )


def joined_along(tiles, dim):
    tiles = jnp.moveaxis(tiles, 0, dim)
    lengths = tiles.shape
    return tiles.reshape(*lengths[:dim], lengths[dim] * lengths[dim + 1], *lengths[dim + 2 :])


def gathered_copies(array, axis, dim):
    tiles = copy_for_each(array, axis)
    return joined_along(tiles, dim)


def over_copies(array, axis):
    return copy_for_each(array, axis).sum(axis=0)


def over_copies_2(array, axis):
    return copy_for_each(array, axis).astype(jnp.float32).sum(axis=0)


def passed_along(array, axis, by):
    devices = lax.axis_size(axis)
    pairs = [(i, i + by) for i in range(devices) if 0 <= i + by < devices]
    return lax.ppermute(array, axis, pairs)


def project(inputs, weights):
    return lax.dot_general(
        inputs, weights, (((1,), (1,)), ((), ())), preferred_element_type=jnp.float32
    )


def convolve(history, current, kernel, tap_mask):
    past_sum = jnp.sum(
        history.astype(jnp.float32) * tap_mask[:, :, None] * kernel[None, :3, :], axis=1
    )
    return jax.nn.silu(past_sum + current * kernel[3][None, :])


def local(
    hidden_in,
    lengths,
    slots,
    norm_gain,
    w_zxo,
    w_bcdt,
    conv_x_weight,
    conv_bc_weight,
    conv_x_pool,
    conv_bc_pool,
    state_pool,
    a_rate,
    dt_bias,
    skip_gain,
    gate_gain,
):
    section_index = lax.axis_index("section")
    section_count = lax.axis_size("section")
    mp_index = lax.axis_index("mp")
    mp_count = lax.axis_size("mp")
    dp_index = lax.axis_index("dp")
    seq_dev = hidden_in.shape[0]
    micro_rows = seq_dev // MICRO
    model_width = norm_gain.shape[1]
    model_share = hidden_in.shape[1]
    heads_dev = a_rate.shape[1]
    head_size = state_pool.shape[3]
    state_size = state_pool.shape[4]
    chan_dev = heads_dev * head_size
    slots_dev = state_pool.shape[1]
    bc_width = conv_bc_weight.shape[2]
    half_width = bc_width // 2
    zxo_rows, small_rows = (
        lax.all_gather(w_zxo, "dp", axis=2, tiled=True),
        lax.all_gather(w_bcdt[:, None], "dp", axis=2, tiled=True),
    )
    proj_weights = lax.all_to_all(zxo_rows, "mp", split_axis=2, concat_axis=3, tiled=True)[0]
    small_full = gathered_copies(small_rows, "mp", 3)[0, 0]
    entry_full = gathered_copies(hidden_in, "mp", 1)
    pre_gain = norm_gain[0]
    post_gain = gate_gain[0]
    kernel_x = conv_x_weight[0]
    kernel_bc = conv_bc_weight[0]
    rate_heads = a_rate[0]
    bias_heads = dt_bias[0]
    skip_heads = skip_gain[0]
    local_slots = slots - dp_index * slots_dev
    tick_count = MICRO + section_count - 1
    hidden_buffer = jnp.zeros((seq_dev, model_share), jnp.bfloat16)
    state_buffer = jnp.zeros((seq_dev, heads_dev, head_size, state_size), jnp.float32)
    received = None
    for tick_index in range(tick_count):
        if tick_index < MICRO:
            first_rows = entry_full[tick_index * micro_rows : (tick_index + 1) * micro_rows]
        else:
            first_rows = jnp.zeros((micro_rows, model_width), jnp.bfloat16)
        if tick_index == 0:
            layer_input = first_rows
        else:
            layer_input = jnp.where(section_index == 0, first_rows, received)
        micro_index = tick_index - section_index
        in_range = (micro_index >= 0) & (micro_index < MICRO)
        row_start = jnp.clip(micro_index, 0, MICRO - 1) * micro_rows
        rows_length = lax.dynamic_slice_in_dim(lengths, row_start, micro_rows)
        rows_slot = lax.dynamic_slice_in_dim(local_slots, row_start, micro_rows)
        tap_mask = (rows_length[:, None] >= (3 - jnp.arange(3, dtype=jnp.int32))[None, :]).astype(
            jnp.float32
        )
        alive = (rows_length > 0).astype(jnp.float32)
        residual = layer_input.astype(jnp.float32)
        normed_in = (
            residual
            * lax.rsqrt(jnp.mean(residual * residual, axis=1, keepdims=True) + epsilon)
            * pre_gain[None, :]
        ).astype(jnp.bfloat16)
        gate_proj = project(normed_in, proj_weights[0])
        inner_proj = project(normed_in, proj_weights[1])
        small_proj = project(normed_in, small_full)
        step_raw = lax.dynamic_slice_in_dim(
            small_proj, bc_width + mp_index * heads_dev, heads_dev, 1
        )
        conv_x = convolve(
            jnp.take(conv_x_pool[0], rows_slot, axis=0), inner_proj, kernel_x, tap_mask
        )
        conv_bc = convolve(
            jnp.take(conv_bc_pool[0], rows_slot, axis=0),
            small_proj[:, :bc_width],
            kernel_bc,
            tap_mask,
        )
        conv_b = conv_bc[:, :half_width]
        conv_c = conv_bc[:, half_width:]
        step_size = jax.nn.softplus(step_raw + bias_heads[None, :])
        decay_rate = jnp.exp(-step_size * rate_heads[None, :])
        old_state = jnp.take(state_pool[0], rows_slot, axis=0) * alive[:, None, None, None]
        inner_heads = conv_x.reshape(micro_rows, heads_dev, head_size)
        new_state = (
            decay_rate[:, :, None, None] * old_state
            + (step_size[:, :, None] * inner_heads)[:, :, :, None] * conv_b[:, None, None, :]
        )
        read_out = (
            jnp.einsum("bhpn,bn->bhp", new_state, conv_c, precision=lax.Precision.HIGHEST)
            + skip_heads[None, :, None] * inner_heads
        )
        gated = read_out.reshape(micro_rows, chan_dev) * jax.nn.silu(gate_proj)
        square_sum = over_copies(jnp.sum(gated * gated, axis=1), "mp")
        normed = (
            gated
            * lax.rsqrt(square_sum[:, None] / (chan_dev * mp_count) + epsilon)
            * post_gain[None, :]
        ).astype(jnp.bfloat16)
        partial_value = jnp.dot(normed, proj_weights[2], preferred_element_type=jnp.float32)
        summed = over_copies_2(partial_value.astype(jnp.bfloat16), "mp").astype(jnp.float32)
        new_full = (residual + summed).astype(jnp.bfloat16)
        new_share = lax.dynamic_slice_in_dim(new_full, mp_index * model_share, model_share, 1)
        current_hidden = lax.dynamic_slice_in_dim(hidden_buffer, row_start, micro_rows, 0)
        hidden_buffer = lax.dynamic_update_slice_in_dim(
            hidden_buffer, jnp.where(in_range, new_share, current_hidden), row_start, 0
        )
        current_state = lax.dynamic_slice_in_dim(state_buffer, row_start, micro_rows, 0)
        state_buffer = lax.dynamic_update_slice_in_dim(
            state_buffer, jnp.where(in_range, new_state, current_state), row_start, 0
        )
        if tick_index + 1 < tick_count:
            received = passed_along(new_full, "section", 1)
    return (hidden_buffer[None], state_buffer[None])


def solution(mesh):
    placed = (
        P("dp", "mp"),
        P("dp"),
        P("dp"),
        P("section", None),
        P("section", None, "dp", "mp"),
        P("section", "dp", "mp"),
        P("section", None, "mp"),
        P("section", None, None),
        P("section", "dp", None, "mp"),
        P("section", "dp", None, None),
        P("section", "dp", "mp", None, None),
        P("section", "mp"),
        P("section", "mp"),
        P("section", "mp"),
        P("section", "mp"),
    )
    return jax.shard_map(
        local,
        mesh=mesh,
        in_specs=placed,
        out_specs=(P("section", "dp", "mp"), P("section", "dp", "mp", None, None)),
        check_vma=False,
    )
```

profile of v0, /device:TPU:128, one launch (start us, length us, event | category | flops | bytes accessed | tf_op | source)
XLA Modules:
  0.0 585.2 jit_solution(429785838524593616)
XLA Ops:
  9.4 5.8 all-to-all-start
  16.1 13.6 %all-gather = bf16[1,336,160]{2,0,1:T(2,128)(2,1)S(1)} all-gather(bf16[1,84,160]{2,0,1:T(2,128)(2,1)S(1)} %copy.74), channel_id=2, replica_groups=mesh['dp'=4,'mp'=16,'section'=4] {'dp'}, dimensions={1}, use_global_device_ids=true | all-gather | bytes 134400 | tf_op jit(solution)/shard_map/all_gather | solution.py:90
  31.4 8.1 %all-to-all-start.1 = ((bf16[16,1,1,336,160]{3,4,2,1,0:T(8,128)(2,1)}), bf16[16,1,1,336,160]{3,4,2,1,0:T(8,128)(2,1)}, u32[]{:S(2)}, u32[]{:S(2)}) async-start(bf16[16,1,1,336,160]{3,4,2,1,0:T(8,128)(2,1)} %broadcast_in_dim.79), calls=%async_computation.1 | async-start | bytes 3932160 | tf_op jit(solution)/shard_map/all_to_all | solution.py:12
  39.5 29.2 %all-gather.3.cloned.1.call-done = bf16[1,3,5120,160]{2,3,1,0:T(8,128)(2,1)} async-done(((bf16[1,3,1280,160]{2,3,1,0:T(8,128)(2,1)}), bf16[1,3,5120,160]{2,3,1,0:T(8,128)(2,1)}) %all-gather.3.cloned.1.call-update) | async-done | bytes 4915216 | tf_op jit(solution)/shard_map/all_gather | solution.py:89
  68.6 15.5 %copy.76 = bf16[1,3,5120,160]{3,1,0,2:T(4,128)(2,1)} copy(bf16[1,3,5120,160]{2,3,1,0:T(8,128)(2,1)} %all-gather.3.cloned.1.call-done) | data formatting | bytes 9830400 | tf_op jit(solution)/shard_map/all_gather | solution.py:89
  84.1 17.6 %reshape.822 = bf16[16,2,76800]{2,1,0:T(2,128)(2,1)} reshape(bf16[5120,1,3,160]{3,2,1,0:T(4,128)(2,1)} %bitcast.134) | data formatting | bytes 9830400
  101.8 5.7 all-to-all-start.2
  117.6 101.7 %all-to-all-done.2 = bf16[16,2,76800]{2,1,0:T(2,128)(2,1)} async-done(((bf16[16,2,76800]{2,1,0:T(2,128)(2,1)}), bf16[16,2,76800]{2,1,0:T(2,128)(2,1)}, u32[]{:S(2)}, u32[]{:S(2)}) %all-to-all-start.2) | async-done | bytes 4915232 | tf_op jit(solution)/shard_map/all_to_all | solution.py:92
  219.2 17.3 %reshape.823 = bf16[5120,1,3,160]{3,2,1,0:T(4,128)(2,1)} reshape(bf16[16,2,76800]{2,1,0:T(2,128)(2,1)} %all-to-all-done.2) | data formatting | bytes 9830400
  236.5 17.8 %copy.77 = bf16[1,3,16,320,160]{3,4,2,1,0:T(8,128)(2,1)} copy(bf16[1,3,16,320,160]{4,1,3,2,0:T(4,128)(2,1)} %bitcast.135) | data formatting | bytes 9830400 | tf_op jit(solution)/shard_map/all_to_all | solution.py:92
  254.3 5.2 fusion.188
  271.1 7.1 %all-to-all-done.3 = f32[16,1,4]{2,1,0:T(1,128)S(1)} async-done(((f32[16,1,4]{2,1,0:T(1,128)}), f32[16,1,4]{2,1,0:T(1,128)S(1)}, u32[]{:S(2)}, u32[]{:S(2)}) %all-to-all-start.3) | async-done | bytes 288 | tf_op jit(solution)/shard_map/all_to_all | solution.py:12
  309.9 3.8 collective-permute-done
  322.2 15.1 %all_to_all.102 = f32[16,1,4]{2,1,0:T(1,128)S(1)} all-to-all(f32[16,1,4]{2,1,0:T(1,128)S(1)} %broadcast_in_dim.82), channel_id=1, replica_groups=mesh['dp'=4,'mp'=16,'section'=4] {'mp'}, dimensions={0} | all-to-all | bytes 512 | tf_op jit(solution)/shard_map/all_to_all | solution.py:12
  339.6 12.8 %all_to_all.103 = bf16[16,4,2560]{2,1,0:T(4,128)(2,1)S(1)} all-to-all(bf16[16,4,2560]{2,1,0:T(4,128)(2,1)S(1)} %broadcast_in_dim.83), channel_id=1, replica_groups=mesh['dp'=4,'mp'=16,'section'=4] {'mp'}, dimensions={0} | all-to-all | bytes 655360 | tf_op jit(solution)/shard_map/all_to_all | solution.py:12
  356.2 5.4 collective-permute-done.1
  369.4 11.0 %all_to_all.104 = f32[16,1,4]{2,1,0:T(1,128)S(1)} all-to-all(f32[16,1,4]{2,1,0:T(1,128)S(1)} %broadcast_in_dim.84), channel_id=1, replica_groups=mesh['dp'=4,'mp'=16,'section'=4] {'mp'}, dimensions={0} | all-to-all | bytes 512 | tf_op jit(solution)/shard_map/all_to_all | solution.py:12
  382.7 12.6 %all_to_all.105 = bf16[16,4,2560]{2,1,0:T(4,128)(2,1)S(1)} all-to-all(bf16[16,4,2560]{2,1,0:T(4,128)(2,1)S(1)} %broadcast_in_dim.85), channel_id=1, replica_groups=mesh['dp'=4,'mp'=16,'section'=4] {'mp'}, dimensions={0} | all-to-all | bytes 655360 | tf_op jit(solution)/shard_map/all_to_all | solution.py:12
  399.1 5.4 collective-permute-done.2
  412.3 11.0 %all_to_all.106 = f32[16,1,4]{2,1,0:T(1,128)S(1)} all-to-all(f32[16,1,4]{2,1,0:T(1,128)S(1)} %broadcast_in_dim.86), channel_id=1, replica_groups=mesh['dp'=4,'mp'=16,'section'=4] {'mp'}, dimensions={0} | all-to-all | bytes 512 | tf_op jit(solution)/shard_map/all_to_all | solution.py:12
  434.8 5.1 all-to-all-done.10
  445.1 4.1 collective-permute-done.3
  460.9 7.0 %all-to-all-done.11 = f32[16,1,4]{2,1,0:T(1,128)S(1)} async-done(((f32[16,1,4]{2,1,0:T(1,128)}), f32[16,1,4]{2,1,0:T(1,128)S(1)}, u32[]{:S(2)}, u32[]{:S(2)}) %all-to-all-start.11) | async-done | bytes 288 | tf_op jit(solution)/shard_map/all_to_all | solution.py:12
  470.9 3.7 all-to-all-start.12
  479.6 5.0 all-to-all-done.12
  489.4 4.4 collective-permute-done.4
  504.9 7.6 %all-to-all-done.13 = f32[16,1,4]{2,1,0:T(1,128)S(1)} async-done(((f32[16,1,4]{2,1,0:T(1,128)}), f32[16,1,4]{2,1,0:T(1,128)S(1)}, u32[]{:S(2)}, u32[]{:S(2)}) %all-to-all-start.13) | async-done | bytes 288 | tf_op jit(solution)/shard_map/all_to_all | solution.py:12
  524.0 3.6 copy.142
  531.3 7.0 %collective-permute-done.5 = bf16[4,2560]{1,0:T(4,128)(2,1)S(1)} collective-permute-done((bf16[4,2560]{1,0:T(4,128)(2,1)S(1)}, bf16[4,2560]{1,0:T(4,128)(2,1)S(1)}, u32[]{:S(2)}, u32[]{:S(2)}) %collective-permute-start.5) | collective-permute-done | bytes 20512 | tf_op jit(solution)/shard_map/ppermute | solution.py:39
  547.3 5.9 %all-to-all-start.15 = ((f32[16,1,4]{2,1,0:T(1,128)}), f32[16,1,4]{2,1,0:T(1,128)S(1)}, u32[]{:S(2)}, u32[]{:S(2)}) async-start(f32[16,1,4]{2,1,0:T(1,128)} %broadcast_in_dim.93), calls=%async_computation.15 | async-start | bytes 16384 | tf_op jit(solution)/shard_map/all_to_all | solution.py:12
  555.6 5.4 all-to-all-done.15
  567.6 9.9 %all-to-all-done.16 = bf16[16,4,2560]{2,1,0:T(4,128)(2,1)S(1)} async-done(((bf16[16,4,2560]{2,1,0:T(4,128)(2,1)}), bf16[16,4,2560]{2,1,0:T(4,128)(2,1)S(1)}, u32[]{:S(2)}, u32[]{:S(2)}) %all-to-all-start.16) | async-done | bytes 327712 | tf_op jit(solution)/shard_map/all_to_all | solution.py:12
  (383 shorter events, 179.5 us)
Async XLA Ops:
  7.2 104.1 %copy-start = (f32[1,18,5,64,128]{4,3,2,1,0:T(8,128)S(1)}, f32[1,18,5,64,128]{4,3,2,1,0:T(8,128)}, u32[]{:S(2)}) copy-start(f32[1,18,5,64,128]{4,3,2,1,0:T(8,128)} %param.31) | copy-start | bytes 8847364
  7.2 61.5 %all-gather.3.cloned.1.call-start = ((), (), s32[]{:S(2)}) async-start(), calls=%async_computation.17 | async-start | bytes 6144000 | tf_op jit(solution)/shard_map/all_gather | solution.py:89
  9.4 20.5 %all-to-all-start = ((bf16[16,16,160]{2,1,0:T(8,128)(2,1)}), bf16[16,16,160]{2,1,0:T(8,128)(2,1)S(1)}, u32[]{:S(2)}, u32[]{:S(2)}) async-start(bf16[16,16,160]{2,1,0:T(8,128)(2,1)} %broadcast_in_dim.76), calls=%async_computation | async-start | bytes 262144 | tf_op jit(solution)/shard_map/all_to_all | solution.py:12
  31.4 70.4 %all-to-all-start.1 = ((bf16[16,1,1,336,160]{3,4,2,1,0:T(8,128)(2,1)}), bf16[16,1,1,336,160]{3,4,2,1,0:T(8,128)(2,1)}, u32[]{:S(2)}, u32[]{:S(2)}) async-start(bf16[16,1,1,336,160]{3,4,2,1,0:T(8,128)(2,1)} %broadcast_in_dim.79), calls=%async_computation.1 | async-start | bytes 3932160 | tf_op jit(solution)/shard_map/all_to_all | solution.py:12
  101.8 117.4 %all-to-all-start.2 = ((bf16[16,2,76800]{2,1,0:T(2,128)(2,1)}), bf16[16,2,76800]{2,1,0:T(2,128)(2,1)}, u32[]{:S(2)}, u32[]{:S(2)}) async-start(bf16[16,2,76800]{2,1,0:T(2,128)(2,1)} %reshape.822), calls=%async_computation.2 | async-start | bytes 9830400 | tf_op jit(solution)/shard_map/all_to_all | solution.py:92
  108.4 153.0 %copy-start.59 = (pred[4]{0:T(512)(128)(4,1)}, pred[4]{0:T(512)(128)(4,1)S(1)}, u32[]{:S(2)}) copy-start(pred[4]{0:T(512)(128)(4,1)S(1)} %get-tuple-element.98) | copy-start | bytes 16
  108.4 153.0 %copy-start.71 = (f32[4]{0:T(128)}, f32[4]{0:T(128)S(1)}, u32[]{:S(2)}) copy-start(f32[4]{0:T(128)S(1)} %get-tuple-element.133) | copy-start | bytes 52
  111.2 125.2 %copy-start.18 = (f32[1,1,256]{2,1,0:T(1,128)}, f32[1,1,256]{2,1,0:T(1,128)S(1)}, u32[]{:S(2)}) copy-start(f32[1,1,256]{2,1,0:T(1,128)S(1)} %slice.161) | copy-start | bytes 3076
  113.9 145.7 %copy-start.15 = (f32[320]{0:T(512)}, f32[320]{0:T(512)S(1)}, u32[]{:S(2)}) copy-start(f32[320]{0:T(512)S(1)} %slice_reduce_fusion) | copy-start | bytes 3844
  114.6 187.6 %copy-start.39 = (f32[4,3]{1,0:T(4,128)}, f32[4,3]{1,0:T(4,128)S(1)}, u32[]{:S(2)}) copy-start(f32[4,3]{1,0:T(4,128)S(1)} %get-tuple-element.100) | copy-start | bytes 148
  117.5 143.9 %copy-start.51 = (f32[4,5]{1,0:T(4,128)}, f32[4,5]{1,0:T(4,128)S(1)}, u32[]{:S(2)}) copy-start(f32[4,5]{1,0:T(4,128)S(1)} %get-tuple-element.61) | copy-start | bytes 244
  117.5 143.8 %copy-start.53 = (f32[4,128]{1,0:T(4,128)}, f32[4,128]{1,0:T(4,128)S(1)}, u32[]{:S(2)}) copy-start(f32[4,128]{1,0:T(4,128)S(1)} %get-tuple-element.86) | copy-start | bytes 6148
  266.4 19.0 %copy-start.13 = (bf16[1,18,3,320]{3,2,1,0:T(4,128)(2,1)S(1)}, bf16[1,18,3,320]{3,2,1,0:T(4,128)(2,1)}, u32[]{:S(2)}) copy-start(bf16[1,18,3,320]{3,2,1,0:T(4,128)(2,1)} %param.29) | copy-start | bytes 103684
  266.4 19.7 %copy-start.17 = (bf16[1,18,3,256]{3,2,1,0:T(4,128)(2,1)S(1)}, bf16[1,18,3,256]{3,2,1,0:T(4,128)(2,1)}, u32[]{:S(2)}) copy-start(bf16[1,18,3,256]{3,2,1,0:T(4,128)(2,1)} %param.30) | copy-start | bytes 82948
  266.4 35.8 %copy-start.23 = (f32[3,320]{1,0:T(4,128)S(1)}, f32[3,320]{1,0:T(4,128)}, u32[]{:S(2)}) copy-start(f32[3,320]{1,0:T(4,128)} %copy-done.22) | copy-start | bytes 11524
  267.0 11.2 %all-to-all-start.3 = ((f32[16,1,4]{2,1,0:T(1,128)}), f32[16,1,4]{2,1,0:T(1,128)S(1)}, u32[]{:S(2)}, u32[]{:S(2)}) async-start(f32[16,1,4]{2,1,0:T(1,128)} %broadcast_in_dim.80), calls=%async_computation.3 | async-start | bytes 16384 | tf_op jit(solution)/shard_map/all_to_all | solution.py:12
  281.2 23.3 %all-to-all-start.4 = ((bf16[16,4,2560]{2,1,0:T(4,128)(2,1)}), bf16[16,4,2560]{2,1,0:T(4,128)(2,1)S(1)}, u32[]{:S(2)}, u32[]{:S(2)}) async-start(bf16[16,4,2560]{2,1,0:T(4,128)(2,1)} %broadcast_in_dim.81), calls=%async_computation.4 | async-start | bytes 655360 | tf_op jit(solution)/shard_map/all_to_all | solution.py:12
  304.7 9.0 %collective-permute-start = (bf16[4,2560]{1,0:T(4,128)(2,1)S(1)}, bf16[4,2560]{1,0:T(4,128)(2,1)S(1)}, u32[]{:S(2)}, u32[]{:S(2)}) collective-permute-start(bf16[4,2560]{1,0:T(4,128)(2,1)S(1)} %add_convert_fusion), channel_id=1, source_target_pairs={{0,1},{1,2},{2,3},{4,5},{5,6},{6,7},{8,9},{9,10},{10,11},{12,13},{... | collective-permute-start | bytes 61448 | tf_op jit(solution)/shard_map/ppermute | solution.py:39
  352.5 9.0 %collective-permute-start.1 = (bf16[4,2560]{1,0:T(4,128)(2,1)S(1)}, bf16[4,2560]{1,0:T(4,128)(2,1)S(1)}, u32[]{:S(2)}, u32[]{:S(2)}) collective-permute-start(bf16[4,2560]{1,0:T(4,128)(2,1)S(1)} %fusion.80), channel_id=1, source_target_pairs={{0,1},{1,2},{2,3},{4,5},{5,6},{6,7},{8,9},{9,10},{10,11},{12,13},{... | collective-permute-start | bytes 61448 | tf_op jit(solution)/shard_map/ppermute | solution.py:39
  395.5 9.0 %collective-permute-start.2 = (bf16[4,2560]{1,0:T(4,128)(2,1)S(1)}, bf16[4,2560]{1,0:T(4,128)(2,1)S(1)}, u32[]{:S(2)}, u32[]{:S(2)}) collective-permute-start(bf16[4,2560]{1,0:T(4,128)(2,1)S(1)} %fusion.84), channel_id=1, source_target_pairs={{0,1},{1,2},{2,3},{4,5},{5,6},{6,7},{8,9},{9,10},{10,11},{12,13},{... | collective-permute-start | bytes 61448 | tf_op jit(solution)/shard_map/ppermute | solution.py:39
  426.4 13.5 %all-to-all-start.10 = ((bf16[16,4,2560]{2,1,0:T(4,128)(2,1)}), bf16[16,4,2560]{2,1,0:T(4,128)(2,1)S(1)}, u32[]{:S(2)}, u32[]{:S(2)}) async-start(bf16[16,4,2560]{2,1,0:T(4,128)(2,1)} %broadcast_in_dim.87), calls=%async_computation.10 | async-start | bytes 655360 | tf_op jit(solution)/shard_map/all_to_all | solution.py:12
  440.1 9.1 %collective-permute-start.3 = (bf16[4,2560]{1,0:T(4,128)(2,1)S(1)}, bf16[4,2560]{1,0:T(4,128)(2,1)S(1)}, u32[]{:S(2)}, u32[]{:S(2)}) collective-permute-start(bf16[4,2560]{1,0:T(4,128)(2,1)S(1)} %fusion.88), channel_id=1, source_target_pairs={{0,1},{1,2},{2,3},{4,5},{5,6},{6,7},{8,9},{9,10},{10,11},{12,13},{... | collective-permute-start | bytes 61448 | tf_op jit(solution)/shard_map/ppermute | solution.py:39
  456.1 18.6 %copy-start.50 = (pred[4]{0:T(512)(128)(4,1)S(1)}, pred[4]{0:T(512)(128)(4,1)}, u32[]{:S(2)}) copy-start(pred[4]{0:T(512)(128)(4,1)} %get-tuple-element.96) | copy-start | bytes 16
  456.1 18.6 %copy-start.56 = (f32[4,5]{1,0:T(4,128)S(1)}, f32[4,5]{1,0:T(4,128)}, u32[]{:S(2)}) copy-start(f32[4,5]{1,0:T(4,128)} %copy-done.55) | copy-start | bytes 244
  456.7 11.2 %all-to-all-start.11 = ((f32[16,1,4]{2,1,0:T(1,128)}), f32[16,1,4]{2,1,0:T(1,128)S(1)}, u32[]{:S(2)}, u32[]{:S(2)}) async-start(f32[16,1,4]{2,1,0:T(1,128)} %broadcast_in_dim.88), calls=%async_computation.11 | async-start | bytes 16384 | tf_op jit(solution)/shard_map/all_to_all | solution.py:12
  470.9 13.6 %all-to-all-start.12 = ((bf16[16,4,2560]{2,1,0:T(4,128)(2,1)}), bf16[16,4,2560]{2,1,0:T(4,128)(2,1)S(1)}, u32[]{:S(2)}, u32[]{:S(2)}) async-start(bf16[16,4,2560]{2,1,0:T(4,128)(2,1)} %broadcast_in_dim.89), calls=%async_computation.12 | async-start | bytes 655360 | tf_op jit(solution)/shard_map/all_to_all | solution.py:12
  484.7 9.1 %collective-permute-start.4 = (bf16[4,2560]{1,0:T(4,128)(2,1)S(1)}, bf16[4,2560]{1,0:T(4,128)(2,1)S(1)}, u32[]{:S(2)}, u32[]{:S(2)}) collective-permute-start(bf16[4,2560]{1,0:T(4,128)(2,1)S(1)} %fusion.92), channel_id=1, source_target_pairs={{0,1},{1,2},{2,3},{4,5},{5,6},{6,7},{8,9},{9,10},{10,11},{12,13},{... | collective-permute-start | bytes 61448 | tf_op jit(solution)/shard_map/ppermute | solution.py:39
  501.3 11.2 %all-to-all-start.13 = ((f32[16,1,4]{2,1,0:T(1,128)}), f32[16,1,4]{2,1,0:T(1,128)S(1)}, u32[]{:S(2)}, u32[]{:S(2)}) async-start(f32[16,1,4]{2,1,0:T(1,128)} %broadcast_in_dim.90), calls=%async_computation.13 | async-start | bytes 16384 | tf_op jit(solution)/shard_map/all_to_all | solution.py:12
  515.6 13.5 %all-to-all-start.14 = ((bf16[16,4,2560]{2,1,0:T(4,128)(2,1)}), bf16[16,4,2560]{2,1,0:T(4,128)(2,1)S(1)}, u32[]{:S(2)}, u32[]{:S(2)}) async-start(bf16[16,4,2560]{2,1,0:T(4,128)(2,1)} %broadcast_in_dim.91), calls=%async_computation.14 | async-start | bytes 655360 | tf_op jit(solution)/shard_map/all_to_all | solution.py:12
  529.3 9.0 %collective-permute-start.5 = (bf16[4,2560]{1,0:T(4,128)(2,1)S(1)}, bf16[4,2560]{1,0:T(4,128)(2,1)S(1)}, u32[]{:S(2)}, u32[]{:S(2)}) collective-permute-start(bf16[4,2560]{1,0:T(4,128)(2,1)S(1)} %fusion.96), channel_id=1, source_target_pairs={{0,1},{1,2},{2,3},{4,5},{5,6},{6,7},{8,9},{9,10},{10,11},{12,13},{... | collective-permute-start | bytes 61448 | tf_op jit(solution)/shard_map/ppermute | solution.py:39
  547.3 13.7 %all-to-all-start.15 = ((f32[16,1,4]{2,1,0:T(1,128)}), f32[16,1,4]{2,1,0:T(1,128)S(1)}, u32[]{:S(2)}, u32[]{:S(2)}) async-start(f32[16,1,4]{2,1,0:T(1,128)} %broadcast_in_dim.93), calls=%async_computation.15 | async-start | bytes 16384 | tf_op jit(solution)/shard_map/all_to_all | solution.py:12
  564.0 13.5 %all-to-all-start.16 = ((bf16[16,4,2560]{2,1,0:T(4,128)(2,1)}), bf16[16,4,2560]{2,1,0:T(4,128)(2,1)S(1)}, u32[]{:S(2)}, u32[]{:S(2)}) async-start(bf16[16,4,2560]{2,1,0:T(4,128)(2,1)} %broadcast_in_dim.94), calls=%async_computation.16 | async-start | bytes 655360 | tf_op jit(solution)/shard_map/all_to_all | solution.py:12
  (63 other events, 403.0 us)
Sparse Core Ops, SparseCore 0:
  9.8 58.7 all-gather.2
where the time goes:
time: 590 us; the launch traced here: 585 us
  waiting for transfers between devices  210 us (36%)
  local copies, waits for them, and re-layouts  122 us (21%)
  blocking collectives  76.2 us (13%)
  starting transfers between devices  65.7 us (11%)
  matrix products  63.9 us (11%)
  other arithmetic  31.3 us (5%)
  between operations  15.4 us (3%)
    all_to_all x1, waiting for transfers between devices, local(): lax.all_to_all(zxo_rows, 'mp', split_axis=2, concat_axis=3, tiled=True)[0]  102 us
    all_to_all x5, blocking collectives, copy_for_each(): lax.all_to_all(jnp.broadcast_to(array[None], (devices, *array.shape)), ax...  62.5 us
    all_to_all x11, waiting for transfers between devices, copy_for_each(): lax.all_to_all(jnp.broadcast_to(array[None], (devices, *array.shape)), ax...  48.7 us
    all_to_all x11, starting transfers between devices, copy_for_each(): lax.all_to_all(jnp.broadcast_to(array[None], (devices, *array.shape)), ax...  48 us
    unnamed x157, local copies, waits for them, and re-layouts  42.3 us
    dot_general x21, matrix products, project(): lax.dot_general(inputs, weights, (((1,), (1,)), ((), ())), preferred_elem...  33 us
    ppermute x6, waiting for transfers between devices, passed_along(): return lax.ppermute(array, axis, pairs)  30.1 us
    all_gather x1, waiting for transfers between devices, local(): lax.all_gather(w_zxo, 'dp', axis=2, tiled=True)  29.2 us
  transfers between devices with their start and end apart: 19, of which 16 were waited for; matrix products, arithmetic and copies ran while one was open for 17% of the time, Pallas kernels for 0%

commit v1 on v0

--- a/solution.py
+++ b/solution.py
@@ -86,7 +86,9 @@
     bc_width = conv_bc_weight.shape[2]
     half_width = bc_width // 2
     zxo_rows, small_rows = (
-        lax.all_gather(w_zxo, "dp", axis=2, tiled=True),
+        jnp.concatenate(
+            lax.all_to_all(jnp.stack([w_zxo] * lax.axis_size("dp")), "dp", 0, 0), axis=2
+        ),
         lax.all_gather(w_bcdt[:, None], "dp", axis=2, tiled=True),
     )
     proj_weights = lax.all_to_all(zxo_rows, "mp", split_axis=2, concat_axis=3, tiled=True)[0]

time: 590 us -> 618 us (1.047)
  blocking collectives: 76.2 us -> 139 us
  waiting for transfers between devices: 210 us -> 191 us
  between operations: 15.4 us -> 1.99 us
    all_gather x1, blocking collectives: 13.6 us -> 62.3 us  [local(): lax.all_gather(w_bcdt[:, None], 'dp', axis=2, tiled=True)]
    all_gather x1 -> x0, waiting for transfers between devices: 29.2 us -> none  [local(): lax.all_gather(w_zxo, 'dp', axis=2, tiled=True)]
    reshape x0 -> x1, local copies, waits for them, and re-layouts: none -> 15.5 us  [local(): jnp.concatenate(lax.all_to_all(jnp.stack([w_zxo] * lax.axis_size('dp')),...]
    all_gather x1 -> x0, local copies, waits for them, and re-layouts: 15.5 us -> none  [local(): lax.all_gather(w_zxo, 'dp', axis=2, tiled=True)]
    all_to_all x5 -> x6, blocking collectives: 62.5 us -> 76.5 us  [copy_for_each(): lax.all_to_all(jnp.broadcast_to(array[None], (devices, *array.shape)), ax...]
    all_to_all x11 -> x10, waiting for transfers between devices: 48.7 us -> 58.7 us  [copy_for_each(): lax.all_to_all(jnp.broadcast_to(array[None], (devices, *array.shape)), ax...]
    all_to_all x11 -> x10, starting transfers between devices: 48 us -> 38.6 us  [copy_for_each(): lax.all_to_all(jnp.broadcast_to(array[None], (devices, *array.shape)), ax...]
    unnamed x157 -> x159, local copies, waits for them, and re-layouts: 42.3 us -> 41.6 us
  transfers between devices with their start and end apart: 19 -> 18, of which waited for: 16 -> 16; matrix products, arithmetic and copies ran while one was open for 17% -> 16% of each run, Pallas kernels for 0% -> 0%
where the time goes in v1:
time: 618 us; the launch traced here: 613 us
  waiting for transfers between devices  191 us (31%)
  blocking collectives  139 us (22%)
  local copies, waits for them, and re-layouts  125 us (20%)
  matrix products  63.9 us (10%)
  starting transfers between devices  60.3 us (10%)
  other arithmetic  31.3 us (5%)
    all_to_all x1, waiting for transfers between devices, local(): lax.all_to_all(zxo_rows, 'mp', split_axis=2, concat_axis=3, tiled=True)[0]  103 us
    all_to_all x6, blocking collectives, copy_for_each(): lax.all_to_all(jnp.broadcast_to(array[None], (devices, *array.shape)), ax...  76.5 us
    all_gather x1, blocking collectives, local(): lax.all_gather(w_bcdt[:, None], 'dp', axis=2, tiled=True)  62.3 us
    all_to_all x10, waiting for transfers between devices, copy_for_each(): lax.all_to_all(jnp.broadcast_to(array[None], (devices, *array.shape)), ax...  58.7 us
    unnamed x159, local copies, waits for them, and re-layouts  41.6 us
    all_to_all x10, starting transfers between devices, copy_for_each(): lax.all_to_all(jnp.broadcast_to(array[None], (devices, *array.shape)), ax...  38.6 us
    dot_general x21, matrix products, project(): lax.dot_general(inputs, weights, (((1,), (1,)), ((), ())), preferred_elem...  33 us
    ppermute x6, waiting for transfers between devices, passed_along(): return lax.ppermute(array, axis, pairs)  30 us
  transfers between devices with their start and end apart: 18, of which 16 were waited for; matrix products, arithmetic and copies ran while one was open for 16% of the time, Pallas kernels for 0%

profile of v1, /device:TPU:128, one launch (start us, length us, event | category | flops | bytes accessed | tf_op | source)
XLA Modules:
  0.0 612.6 jit_solution(11823452913391581471)
XLA Ops:
  1.5 14.1 %all_to_all.107 = bf16[16,16,160]{2,1,0:T(8,128)(2,1)S(1)} all-to-all(bf16[16,16,160]{2,1,0:T(8,128)(2,1)S(1)} %broadcast_in_dim.76), channel_id=1, replica_groups=mesh['dp'=4,'mp'=16,'section'=4] {'mp'}, dimensions={0} | all-to-all | bytes 163840 | tf_op jit(solution)/shard_map/all_to_all | solution.py:12
  15.6 3.9 stack.2
  19.5 5.1 all-to-all-start.2
  24.8 62.3 %all-gather = bf16[1,336,160]{2,0,1:T(2,128)(2,1)S(1)} all-gather(bf16[1,84,160]{2,0,1:T(2,128)(2,1)S(1)} %copy.70), channel_id=2, replica_groups=mesh['dp'=4,'mp'=16,'section'=4] {'dp'}, dimensions={1}, use_global_device_ids=true | all-gather | bytes 134400 | tf_op jit(solution)/shard_map/all_gather | solution.py:92
  88.8 4.4 all-to-all-start.1
  93.2 15.5 %copy.103 = bf16[1,3,4,1280,160]{4,1,3,2,0:T(4,128)(2,1)} copy(bf16[1,3,4,1280,160]{3,4,1,0,2:T(8,128)(2,1)} %bitcast.10) | data formatting | bytes 9830400 | tf_op jit(solution)/shard_map/reshape | solution.py:89
  108.7 17.6 %reshape.833 = bf16[16,2,76800]{2,1,0:T(2,128)(2,1)} reshape(bf16[5120,1,3,160]{3,2,1,0:T(4,128)(2,1)} %bitcast.137) | data formatting | bytes 9830400
  126.4 10.1 %all-to-all-done.1 = bf16[16,1,1,336,160]{3,4,2,1,0:T(8,128)(2,1)} async-done(((bf16[16,1,1,336,160]{3,4,2,1,0:T(8,128)(2,1)}), bf16[16,1,1,336,160]{3,4,2,1,0:T(8,128)(2,1)}, u32[]{:S(2)}, u32[]{:S(2)}) %all-to-all-start.1) | async-done | bytes 1720352 | tf_op jit(solution)/shard_map/all_to_all | solution.py:12
  136.5 4.6 all-to-all-start.3
  151.2 102.5 %all-to-all-done.3 = bf16[16,2,76800]{2,1,0:T(2,128)(2,1)} async-done(((bf16[16,2,76800]{2,1,0:T(2,128)(2,1)}), bf16[16,2,76800]{2,1,0:T(2,128)(2,1)}, u32[]{:S(2)}, u32[]{:S(2)}) %all-to-all-start.3) | async-done | bytes 4915232 | tf_op jit(solution)/shard_map/all_to_all | solution.py:94
  253.7 17.3 %reshape.834 = bf16[5120,1,3,160]{3,2,1,0:T(4,128)(2,1)} reshape(bf16[16,2,76800]{2,1,0:T(2,128)(2,1)} %all-to-all-done.3) | data formatting | bytes 9830400
  271.0 17.8 %copy.74 = bf16[1,3,16,320,160]{3,4,2,1,0:T(8,128)(2,1)} copy(bf16[1,3,16,320,160]{4,1,3,2,0:T(4,128)(2,1)} %bitcast.138) | data formatting | bytes 9830400 | tf_op jit(solution)/shard_map/all_to_all | solution.py:94
  288.8 5.2 fusion.188
  305.6 7.1 %all-to-all-done.4 = f32[16,1,4]{2,1,0:T(1,128)S(1)} async-done(((f32[16,1,4]{2,1,0:T(1,128)}), f32[16,1,4]{2,1,0:T(1,128)S(1)}, u32[]{:S(2)}, u32[]{:S(2)}) %all-to-all-start.4) | async-done | bytes 288 | tf_op jit(solution)/shard_map/all_to_all | solution.py:12
  344.4 3.8 collective-permute-done
  356.6 15.1 %all_to_all.108 = f32[16,1,4]{2,1,0:T(1,128)S(1)} all-to-all(f32[16,1,4]{2,1,0:T(1,128)S(1)} %broadcast_in_dim.82), channel_id=1, replica_groups=mesh['dp'=4,'mp'=16,'section'=4] {'mp'}, dimensions={0} | all-to-all | bytes 512 | tf_op jit(solution)/shard_map/all_to_all | solution.py:12
  374.1 12.6 %all_to_all.109 = bf16[16,4,2560]{2,1,0:T(4,128)(2,1)S(1)} all-to-all(bf16[16,4,2560]{2,1,0:T(4,128)(2,1)S(1)} %broadcast_in_dim.83), channel_id=1, replica_groups=mesh['dp'=4,'mp'=16,'section'=4] {'mp'}, dimensions={0} | all-to-all | bytes 655360 | tf_op jit(solution)/shard_map/all_to_all | solution.py:12
  390.5 5.3 collective-permute-done.1
  403.7 11.0 %all_to_all.110 = f32[16,1,4]{2,1,0:T(1,128)S(1)} all-to-all(f32[16,1,4]{2,1,0:T(1,128)S(1)} %broadcast_in_dim.84), channel_id=1, replica_groups=mesh['dp'=4,'mp'=16,'section'=4] {'mp'}, dimensions={0} | all-to-all | bytes 512 | tf_op jit(solution)/shard_map/all_to_all | solution.py:12
  417.0 12.6 %all_to_all.111 = bf16[16,4,2560]{2,1,0:T(4,128)(2,1)S(1)} all-to-all(bf16[16,4,2560]{2,1,0:T(4,128)(2,1)S(1)} %broadcast_in_dim.85), channel_id=1, replica_groups=mesh['dp'=4,'mp'=16,'section'=4] {'mp'}, dimensions={0} | all-to-all | bytes 655360 | tf_op jit(solution)/shard_map/all_to_all | solution.py:12
  433.3 5.4 collective-permute-done.2
  446.6 11.0 %all_to_all.112 = f32[16,1,4]{2,1,0:T(1,128)S(1)} all-to-all(f32[16,1,4]{2,1,0:T(1,128)S(1)} %broadcast_in_dim.86), channel_id=1, replica_groups=mesh['dp'=4,'mp'=16,'section'=4] {'mp'}, dimensions={0} | all-to-all | bytes 512 | tf_op jit(solution)/shard_map/all_to_all | solution.py:12
  469.1 5.0 all-to-all-done.11
  479.4 4.1 collective-permute-done.3
  495.2 7.0 %all-to-all-done.12 = f32[16,1,4]{2,1,0:T(1,128)S(1)} async-done(((f32[16,1,4]{2,1,0:T(1,128)}), f32[16,1,4]{2,1,0:T(1,128)S(1)}, u32[]{:S(2)}, u32[]{:S(2)}) %all-to-all-start.12) | async-done | bytes 288 | tf_op jit(solution)/shard_map/all_to_all | solution.py:12
  513.8 5.0 all-to-all-done.13
  523.7 4.4 collective-permute-done.4
  539.2 7.6 %all-to-all-done.14 = f32[16,1,4]{2,1,0:T(1,128)S(1)} async-done(((f32[16,1,4]{2,1,0:T(1,128)}), f32[16,1,4]{2,1,0:T(1,128)S(1)}, u32[]{:S(2)}, u32[]{:S(2)}) %all-to-all-start.14) | async-done | bytes 288 | tf_op jit(solution)/shard_map/all_to_all | solution.py:12
  565.6 7.0 %collective-permute-done.5 = bf16[4,2560]{1,0:T(4,128)(2,1)S(1)} collective-permute-done((bf16[4,2560]{1,0:T(4,128)(2,1)S(1)}, bf16[4,2560]{1,0:T(4,128)(2,1)S(1)}, u32[]{:S(2)}, u32[]{:S(2)}) %collective-permute-start.5) | collective-permute-done | bytes 20512 | tf_op jit(solution)/shard_map/ppermute | solution.py:39
  581.5 5.9 all-to-all-start.16
  589.9 5.4 all-to-all-done.16
  601.9 9.9 %all-to-all-done.17 = bf16[16,4,2560]{2,1,0:T(4,128)(2,1)S(1)} async-done(((bf16[16,4,2560]{2,1,0:T(4,128)(2,1)}), bf16[16,4,2560]{2,1,0:T(4,128)(2,1)S(1)}, u32[]{:S(2)}, u32[]{:S(2)}) %all-to-all-start.17) | async-done | bytes 327712 | tf_op jit(solution)/shard_map/all_to_all | solution.py:12
  (384 shorter events, 184.7 us)
Async XLA Ops:
  0.6 144.2 %copy-start = (f32[1,18,5,64,128]{4,3,2,1,0:T(8,128)S(1)}, f32[1,18,5,64,128]{4,3,2,1,0:T(8,128)}, u32[]{:S(2)}) copy-start(f32[1,18,5,64,128]{4,3,2,1,0:T(8,128)} %param.31) | copy-start | bytes 8847364
  19.5 67.8 %all-to-all-start.2 = ((bf16[4,1,3,1280,160]{3,4,2,1,0:T(8,128)(2,1)}), bf16[4,1,3,1280,160]{3,4,2,1,0:T(8,128)(2,1)}, u32[]{:S(2)}, u32[]{:S(2)}) async-start(bf16[4,1,3,1280,160]{3,4,2,1,0:T(8,128)(2,1)} %stack.2), calls=%async_computation.2 | async-start | bytes 9830400 | tf_op jit(solution)/shard_map/all_to_all | solution.py:90
  88.8 47.7 %all-to-all-start.1 = ((bf16[16,1,1,336,160]{3,4,2,1,0:T(8,128)(2,1)}), bf16[16,1,1,336,160]{3,4,2,1,0:T(8,128)(2,1)}, u32[]{:S(2)}, u32[]{:S(2)}) async-start(bf16[16,1,1,336,160]{3,4,2,1,0:T(8,128)(2,1)} %broadcast_in_dim.79), calls=%async_computation.1 | async-start | bytes 3932160 | tf_op jit(solution)/shard_map/all_to_all | solution.py:12
  126.4 21.1 %copy-start.44 = (f32[1,4,320]{2,1,0:T(4,128)S(1)}, f32[1,4,320]{2,1,0:T(4,128)}, u32[]{:S(2)}) copy-start(f32[1,4,320]{2,1,0:T(4,128)} %param.27) | copy-start | bytes 15364
  136.5 117.2 %all-to-all-start.3 = ((bf16[16,2,76800]{2,1,0:T(2,128)(2,1)}), bf16[16,2,76800]{2,1,0:T(2,128)(2,1)}, u32[]{:S(2)}, u32[]{:S(2)}) async-start(bf16[16,2,76800]{2,1,0:T(2,128)(2,1)} %reshape.833), calls=%async_computation.3 | async-start | bytes 9830400 | tf_op jit(solution)/shard_map/all_to_all | solution.py:94
  142.0 153.8 %copy-start.60 = (pred[4]{0:T(512)(128)(4,1)}, pred[4]{0:T(512)(128)(4,1)S(1)}, u32[]{:S(2)}) copy-start(pred[4]{0:T(512)(128)(4,1)S(1)} %get-tuple-element.98) | copy-start | bytes 16
  142.1 153.8 %copy-start.72 = (f32[4]{0:T(128)}, f32[4]{0:T(128)S(1)}, u32[]{:S(2)}) copy-start(f32[4]{0:T(128)S(1)} %get-tuple-element.133) | copy-start | bytes 52
  144.9 126.1 %copy-start.18 = (f32[1,1,256]{2,1,0:T(1,128)}, f32[1,1,256]{2,1,0:T(1,128)S(1)}, u32[]{:S(2)}) copy-start(f32[1,1,256]{2,1,0:T(1,128)S(1)} %slice.161) | copy-start | bytes 3076
  147.5 146.5 %copy-start.15 = (f32[320]{0:T(512)}, f32[320]{0:T(512)S(1)}, u32[]{:S(2)}) copy-start(f32[320]{0:T(512)S(1)} %slice_reduce_fusion) | copy-start | bytes 3844
  148.2 188.4 %copy-start.40 = (f32[4,3]{1,0:T(4,128)}, f32[4,3]{1,0:T(4,128)S(1)}, u32[]{:S(2)}) copy-start(f32[4,3]{1,0:T(4,128)S(1)} %get-tuple-element.100) | copy-start | bytes 148
  151.2 144.7 %copy-start.52 = (f32[4,5]{1,0:T(4,128)}, f32[4,5]{1,0:T(4,128)S(1)}, u32[]{:S(2)}) copy-start(f32[4,5]{1,0:T(4,128)S(1)} %get-tuple-element.61) | copy-start | bytes 244
  151.2 144.7 %copy-start.54 = (f32[4,128]{1,0:T(4,128)}, f32[4,128]{1,0:T(4,128)S(1)}, u32[]{:S(2)}) copy-start(f32[4,128]{1,0:T(4,128)S(1)} %get-tuple-element.86) | copy-start | bytes 6148
  300.9 19.0 %copy-start.13 = (bf16[1,18,3,320]{3,2,1,0:T(4,128)(2,1)S(1)}, bf16[1,18,3,320]{3,2,1,0:T(4,128)(2,1)}, u32[]{:S(2)}) copy-start(bf16[1,18,3,320]{3,2,1,0:T(4,128)(2,1)} %param.29) | copy-start | bytes 103684
  300.9 19.7 %copy-start.17 = (bf16[1,18,3,256]{3,2,1,0:T(4,128)(2,1)S(1)}, bf16[1,18,3,256]{3,2,1,0:T(4,128)(2,1)}, u32[]{:S(2)}) copy-start(bf16[1,18,3,256]{3,2,1,0:T(4,128)(2,1)} %param.30) | copy-start | bytes 82948
  300.9 35.7 %copy-start.23 = (f32[3,320]{1,0:T(4,128)S(1)}, f32[3,320]{1,0:T(4,128)}, u32[]{:S(2)}) copy-start(f32[3,320]{1,0:T(4,128)} %copy-done.22) | copy-start | bytes 11524
  301.5 11.2 %all-to-all-start.4 = ((f32[16,1,4]{2,1,0:T(1,128)}), f32[16,1,4]{2,1,0:T(1,128)S(1)}, u32[]{:S(2)}, u32[]{:S(2)}) async-start(f32[16,1,4]{2,1,0:T(1,128)} %broadcast_in_dim.80), calls=%async_computation.4 | async-start | bytes 16384 | tf_op jit(solution)/shard_map/all_to_all | solution.py:12
  315.8 23.2 %all-to-all-start.5 = ((bf16[16,4,2560]{2,1,0:T(4,128)(2,1)}), bf16[16,4,2560]{2,1,0:T(4,128)(2,1)S(1)}, u32[]{:S(2)}, u32[]{:S(2)}) async-start(bf16[16,4,2560]{2,1,0:T(4,128)(2,1)} %broadcast_in_dim.81), calls=%async_computation.5 | async-start | bytes 655360 | tf_op jit(solution)/shard_map/all_to_all | solution.py:12
  339.2 9.0 %collective-permute-start = (bf16[4,2560]{1,0:T(4,128)(2,1)S(1)}, bf16[4,2560]{1,0:T(4,128)(2,1)S(1)}, u32[]{:S(2)}, u32[]{:S(2)}) collective-permute-start(bf16[4,2560]{1,0:T(4,128)(2,1)S(1)} %add_convert_fusion), channel_id=1, source_target_pairs={{0,1},{1,2},{2,3},{4,5},{5,6},{6,7},{8,9},{9,10},{10,11},{12,13},{... | collective-permute-start | bytes 61448 | tf_op jit(solution)/shard_map/ppermute | solution.py:39
  386.8 9.0 %collective-permute-start.1 = (bf16[4,2560]{1,0:T(4,128)(2,1)S(1)}, bf16[4,2560]{1,0:T(4,128)(2,1)S(1)}, u32[]{:S(2)}, u32[]{:S(2)}) collective-permute-start(bf16[4,2560]{1,0:T(4,128)(2,1)S(1)} %fusion.80), channel_id=1, source_target_pairs={{0,1},{1,2},{2,3},{4,5},{5,6},{6,7},{8,9},{9,10},{10,11},{12,13},{... | collective-permute-start | bytes 61448 | tf_op jit(solution)/shard_map/ppermute | solution.py:39
  429.7 9.0 %collective-permute-start.2 = (bf16[4,2560]{1,0:T(4,128)(2,1)S(1)}, bf16[4,2560]{1,0:T(4,128)(2,1)S(1)}, u32[]{:S(2)}, u32[]{:S(2)}) collective-permute-start(bf16[4,2560]{1,0:T(4,128)(2,1)S(1)} %fusion.84), channel_id=1, source_target_pairs={{0,1},{1,2},{2,3},{4,5},{5,6},{6,7},{8,9},{9,10},{10,11},{12,13},{... | collective-permute-start | bytes 61448 | tf_op jit(solution)/shard_map/ppermute | solution.py:39
  460.7 13.5 %all-to-all-start.11 = ((bf16[16,4,2560]{2,1,0:T(4,128)(2,1)}), bf16[16,4,2560]{2,1,0:T(4,128)(2,1)S(1)}, u32[]{:S(2)}, u32[]{:S(2)}) async-start(bf16[16,4,2560]{2,1,0:T(4,128)(2,1)} %broadcast_in_dim.87), calls=%async_computation.11 | async-start | bytes 655360 | tf_op jit(solution)/shard_map/all_to_all | solution.py:12
  474.3 9.1 %collective-permute-start.3 = (bf16[4,2560]{1,0:T(4,128)(2,1)S(1)}, bf16[4,2560]{1,0:T(4,128)(2,1)S(1)}, u32[]{:S(2)}, u32[]{:S(2)}) collective-permute-start(bf16[4,2560]{1,0:T(4,128)(2,1)S(1)} %fusion.88), channel_id=1, source_target_pairs={{0,1},{1,2},{2,3},{4,5},{5,6},{6,7},{8,9},{9,10},{10,11},{12,13},{... | collective-permute-start | bytes 61448 | tf_op jit(solution)/shard_map/ppermute | solution.py:39
  490.3 18.6 %copy-start.51 = (pred[4]{0:T(512)(128)(4,1)S(1)}, pred[4]{0:T(512)(128)(4,1)}, u32[]{:S(2)}) copy-start(pred[4]{0:T(512)(128)(4,1)} %get-tuple-element.96) | copy-start | bytes 16
  490.3 18.6 %copy-start.57 = (f32[4,5]{1,0:T(4,128)S(1)}, f32[4,5]{1,0:T(4,128)}, u32[]{:S(2)}) copy-start(f32[4,5]{1,0:T(4,128)} %copy-done.56) | copy-start | bytes 244
  491.0 11.2 %all-to-all-start.12 = ((f32[16,1,4]{2,1,0:T(1,128)}), f32[16,1,4]{2,1,0:T(1,128)S(1)}, u32[]{:S(2)}, u32[]{:S(2)}) async-start(f32[16,1,4]{2,1,0:T(1,128)} %broadcast_in_dim.88), calls=%async_computation.12 | async-start | bytes 16384 | tf_op jit(solution)/shard_map/all_to_all | solution.py:12
  505.2 13.6 %all-to-all-start.13 = ((bf16[16,4,2560]{2,1,0:T(4,128)(2,1)}), bf16[16,4,2560]{2,1,0:T(4,128)(2,1)S(1)}, u32[]{:S(2)}, u32[]{:S(2)}) async-start(bf16[16,4,2560]{2,1,0:T(4,128)(2,1)} %broadcast_in_dim.89), calls=%async_computation.13 | async-start | bytes 655360 | tf_op jit(solution)/shard_map/all_to_all | solution.py:12
  519.0 9.1 %collective-permute-start.4 = (bf16[4,2560]{1,0:T(4,128)(2,1)S(1)}, bf16[4,2560]{1,0:T(4,128)(2,1)S(1)}, u32[]{:S(2)}, u32[]{:S(2)}) collective-permute-start(bf16[4,2560]{1,0:T(4,128)(2,1)S(1)} %fusion.92), channel_id=1, source_target_pairs={{0,1},{1,2},{2,3},{4,5},{5,6},{6,7},{8,9},{9,10},{10,11},{12,13},{... | collective-permute-start | bytes 61448 | tf_op jit(solution)/shard_map/ppermute | solution.py:39
  535.6 11.2 %all-to-all-start.14 = ((f32[16,1,4]{2,1,0:T(1,128)}), f32[16,1,4]{2,1,0:T(1,128)S(1)}, u32[]{:S(2)}, u32[]{:S(2)}) async-start(f32[16,1,4]{2,1,0:T(1,128)} %broadcast_in_dim.90), calls=%async_computation.14 | async-start | bytes 16384 | tf_op jit(solution)/shard_map/all_to_all | solution.py:12
  549.9 13.5 %all-to-all-start.15 = ((bf16[16,4,2560]{2,1,0:T(4,128)(2,1)}), bf16[16,4,2560]{2,1,0:T(4,128)(2,1)S(1)}, u32[]{:S(2)}, u32[]{:S(2)}) async-start(bf16[16,4,2560]{2,1,0:T(4,128)(2,1)} %broadcast_in_dim.91), calls=%async_computation.15 | async-start | bytes 655360 | tf_op jit(solution)/shard_map/all_to_all | solution.py:12
  563.5 9.0 %collective-permute-start.5 = (bf16[4,2560]{1,0:T(4,128)(2,1)S(1)}, bf16[4,2560]{1,0:T(4,128)(2,1)S(1)}, u32[]{:S(2)}, u32[]{:S(2)}) collective-permute-start(bf16[4,2560]{1,0:T(4,128)(2,1)S(1)} %fusion.96), channel_id=1, source_target_pairs={{0,1},{1,2},{2,3},{4,5},{5,6},{6,7},{8,9},{9,10},{10,11},{12,13},{... | collective-permute-start | bytes 61448 | tf_op jit(solution)/shard_map/ppermute | solution.py:39
  581.5 13.7 %all-to-all-start.16 = ((f32[16,1,4]{2,1,0:T(1,128)}), f32[16,1,4]{2,1,0:T(1,128)S(1)}, u32[]{:S(2)}, u32[]{:S(2)}) async-start(f32[16,1,4]{2,1,0:T(1,128)} %broadcast_in_dim.93), calls=%async_computation.16 | async-start | bytes 16384 | tf_op jit(solution)/shard_map/all_to_all | solution.py:12
  598.3 13.5 %all-to-all-start.17 = ((bf16[16,4,2560]{2,1,0:T(4,128)(2,1)}), bf16[16,4,2560]{2,1,0:T(4,128)(2,1)S(1)}, u32[]{:S(2)}, u32[]{:S(2)}) async-start(bf16[16,4,2560]{2,1,0:T(4,128)(2,1)} %broadcast_in_dim.94), calls=%async_computation.17 | async-start | bytes 655360 | tf_op jit(solution)/shard_map/all_to_all | solution.py:12
  (63 other events, 432.2 us)
